TPU v7x, 32 devices: a whole 2x2x4 slice. The times are simulated.
32 devices in a mesh: wide: 2 (over x), grow: 4 (over y, core), gcol: 4 (over z).
Axes of the slice: x: 2, y: 2, z: 4, core: 2. Of those that a mesh axis runs over, the one named last changes fastest.
Arguments:
- diag_block: float32 [2, 1024, 1024], P('wide', ('grow', 'gcol')), as said below
- lower_block: float32 [2, 3072, 1024], P('wide', ('grow', 'gcol')), may hold values from -0.1875 to 0.1875
- trailing_block: float32 [2, 3072, 3072], P('wide', 'grow', 'gcol'), as said below
- parent_front: float32 [4, 2048, 8192], P('grow', 'wide', 'gcol'), may hold values from -3 to 3
- row_map: int32 [2, 24], replicated, may hold values from 0 to 63, as said below
Outputs:
- factor: float32 [2, 1024, 1024], P('wide', ('grow', 'gcol'))
- panel: float32 [2, 3072, 1024], P('wide', ('grow', 'gcol'))
- parent: float32 [4, 2048, 8192], P('grow', 'wide', 'gcol')
Inputs may be any that keep to these rules, and one draw needn't show every extreme that they name: Each diag_block[g] is symmetric and positive definite. Each trailing_block[g] is symmetric. `row_map`: the blocks of one child are distinct, and child block b goes to a grandparent block p with p // 16 equal to b // 6.
All inputs are finite; a program needn't handle non-finite values.
Results may differ from a plain program's by a relative error of at most 0.0003.
Values sent between devices are 32-bit elements; how exact they have to be, the bound alone decides.
A program may use at most 128 MiB of HBM per device.

v0:
```python
import functools

import jax
import jax.numpy as jnp
from jax import lax
from jax.experimental import pallas as pl
from jax.experimental.pallas import tpu as pltpu
from jax.sharding import PartitionSpec as P

BLOCK = 128
HALF = 64
F32 = jnp.float32
BF16 = jnp.bfloat16
NT = (((1,), (1,)), ((), ()))
NN = (((1,), (0,)), ((), ()))
VMEM = pl.BlockSpec(memory_space=pltpu.VMEM)
SMEM = pl.BlockSpec(memory_space=pltpu.SMEM)


def full_dot(a, b, dims):
    return lax.dot_general(
        a, b, dims, precision=lax.Precision.HIGHEST, preferred_element_type=F32
    )


def parts(x):
    high = x.astype(BF16)
    return high, (x - high.astype(F32)).astype(BF16)


def split_dot(a, b, dims):
    one = functools.partial(lax.dot_general, dimension_numbers=dims, preferred_element_type=F32)
    return one(a[0], b[0]) + (one(a[0], b[1]) + one(a[1], b[0]))


def factor_half(block):
    half = block.shape[0]
    rows = lax.broadcasted_iota(jnp.int32, (half, half), 0)
    cols = lax.broadcasted_iota(jnp.int32, (half, half), 1)
    eye = jnp.where(rows == cols, 1.0, 0.0).astype(F32)
    full = jnp.concatenate([block, eye], axis=1)
    count = half // 8
    wide = (8, 2 * half)
    groups = [full[8 * s : 8 * s + 8] for s in range(count)]
    sub = lax.broadcasted_iota(jnp.int32, wide, 0)
    done = []
    for s in range(count):
        c = 8 * s
        spread = lambda x: jnp.broadcast_to(x, wide)
        lead = [spread(groups[s][i : i + 1, :]) for i in range(8)]
        pivot = {
            (i, j): spread(lead[i][:, c + j : c + j + 1]) for i in range(8) for j in range(i, 8)
        }
        below = range(s + 1, count)
        column = {t: [spread(groups[t][:, c + j : c + j + 1]) for j in range(8)] for t in below}
        keep = jnp.zeros(wide, F32)
        for j in range(8):
            r = lax.rsqrt(pivot[j, j])
            unit = lead[j] * r
            mult = {i: pivot[j, i] * r for i in range(j + 1, 8)}
            for i in range(j + 1, 8):
                for q in range(i, 8):
                    pivot[i, q] = pivot[i, q] - mult[i] * mult[q]
                lead[i] = lead[i] - mult[i] * unit
            for t in below:
                m = column[t][j] * r
                for i in range(j + 1, 8):
                    column[t][i] = column[t][i] - m * mult[i]
                groups[t] = groups[t] - m * unit
            keep = jnp.where(sub == j, unit, keep)
        done.append(keep)
    both = jnp.concatenate(done, axis=0)
    upper = jnp.where(rows <= cols, both[:, :half], 0.0)
    inverse = jnp.where(rows >= cols, both[:, half:], 0.0)
    return upper.T, inverse


def square(a, b, c):
    return jnp.concatenate(
        [
            jnp.concatenate([a, jnp.zeros_like(a)], axis=1),
            jnp.concatenate([b, c], axis=1),
        ],
        axis=0,
    )


def factor_in_place(a, w, between):
    n = a.shape[0]
    count = n // BLOCK

    def step(k, carry):
        o = pl.multiple_of(k * BLOCK, BLOCK)
        d = a[pl.ds(o, BLOCK), pl.ds(o, BLOCK)]
        l1, w1 = factor_half(d[:HALF, :HALF])
        l21 = full_dot(d[HALF:, :HALF], w1, NT)
        l2, w2 = factor_half(d[HALF:, HALF:] - full_dot(l21, l21, NT))
        w21 = -full_dot(w2, full_dot(l21, w1, NN), NN)
        a[pl.ds(o, BLOCK), pl.ds(o, BLOCK)] = square(l1, l21, l2)
        w[k] = square(w1, w21, w2)
        for at in range(count - 1):

            @pl.when(k == at)
            def _(at=at):
                low, high = at * BLOCK, at * BLOCK + BLOCK
                a[low:high, high:] = jnp.zeros((BLOCK, n - high), F32)
                p = full_dot(a[high:, low:high], w[at], NT)
                a[high:, low:high] = p
                for c in range(high, n, 2 * BLOCK):
                    e = min(c + 2 * BLOCK, n)
                    a[c:, c:e] = a[c:, c:e] - full_dot(p[c - high :], p[c - high : e - high], NT)
                for act in between.get(at, ()):
                    act()

        return carry

    lax.fori_loop(0, count, step, 0)


def gather_factor_kernel(
    rows, columns, d_ref, x_ref, a, w, br, bc,
    local, line_send, line_recv, far_send, far_recv, near_send, near_recv,
    b_send, b_recv, c_send, c_recv,
):
    row, column = lax.axis_index("grow"), lax.axis_index("gcol")
    far_row = lax.rem(row + rows // 2, rows)
    near_row = row + 1 - 2 * lax.rem(row, 2)
    right, left = {"gcol": column + 1}, {"gcol": column - 1}
    far, near = {"grow": far_row}, {"grow": near_row}
    share, part = d_ref.shape[0], x_ref.shape[0]
    has_left, has_right = column > 0, column < columns - 1

    def band(r, c):
        return a.at[pl.ds(pl.multiple_of((r * columns + c) * share, share), share)]

    def piece(ref, c):
        return ref.at[pl.ds(pl.multiple_of(c * part, part), part)]

    def remote(ref, send, recv, to):
        return pltpu.make_async_remote_copy(
            src_ref=ref, dst_ref=ref, send_sem=send, recv_sem=recv,
            device_id=to, device_id_type=pl.DeviceIdType.MESH,
        )

    own_d = pltpu.make_async_copy(d_ref, band(row, column), local.at[0])
    own_x = pltpu.make_async_copy(x_ref, piece(br, column), local.at[1])
    own_d.start()
    own_x.start()
    barrier = pltpu.get_barrier_semaphore()
    next_column = {"gcol": lax.rem(column + 1, columns)}
    last_column = {"gcol": lax.rem(column + columns - 1, columns)}
    for to in (far, near, next_column, last_column):
        pl.semaphore_signal(barrier, inc=1, device_id=to, device_id_type=pl.DeviceIdType.MESH)
    pl.semaphore_wait(barrier, 4)
    own_d.wait()
    own_x.wait()

    def pass_on(ref, send, recv, c, both=False):
        @pl.when((c <= column) & has_right)
        def _():
            remote(ref, send.at[0, c], recv.at[c], right).start()

        @pl.when((c >= column) & has_left)
        def _():
            remote(ref, send.at[1, c], recv.at[c], left).start()

    def passed(ref, send, recv, c):
        @pl.when((c <= column) & has_right)
        def _():
            remote(ref, send.at[0, c], recv.at[c], right).wait_send()

        @pl.when((c >= column) & has_left)
        def _():
            remote(ref, send.at[1, c], recv.at[c], left).wait_send()

    def at_distance(d, act):
        for c, there in ((column - d, column - d >= 0), (column + d, column + d < columns)):
            pl.when(there)(functools.partial(act, c))

    def spread(c):
        remote(band(row, c), far_send.at[c], far_recv.at[c], far).start()
        remote(band(row, c), near_send.at[0, c], near_recv.at[0, c], near).start()

    pass_on(band(row, column), line_send, line_recv, column)
    spread(column)

    def arrived(c):
        remote(band(row, c), line_send.at[0, c], line_recv.at[c], right).wait_recv()
        pass_on(band(row, c), line_send, line_recv, c)
        spread(c)

    def crossed(c):
        remote(band(far_row, c), far_send.at[c], far_recv.at[c], far).wait_recv()
        remote(band(far_row, c), near_send.at[1, c], near_recv.at[1, c], near).start()

    at_distance(1, arrived)
    crossed(column)
    for d in range(2, columns):
        at_distance(d, arrived)
        at_distance(d - 1, crossed)
    pass_on(piece(br, column), b_send, b_recv, column)
    at_distance(columns - 1, crossed)
    near_far_row = lax.rem(near_row + rows // 2, rows)
    for c in range(columns):
        remote(band(near_row, c), near_send.at[0, c], near_recv.at[0, c], near).wait_recv()
        remote(band(near_far_row, c), near_send.at[1, c], near_recv.at[1, c], near).wait_recv()
    for c in range(columns):
        remote(band(row, c), far_send.at[c], far_recv.at[c], far).wait_send()
        remote(band(row, c), near_send.at[0, c], near_recv.at[0, c], near).wait_send()
        remote(band(far_row, c), near_send.at[1, c], near_recv.at[1, c], near).wait_send()
        passed(band(row, c), line_send, line_recv, c)

    root = row == column
    relay = far_row == column
    from_far = relay
    from_near = jnp.logical_not(root | relay)

    def give(c):
        @pl.when(root)
        def _():
            for slot, to in ((0, far), (1, near)):
                pltpu.make_async_remote_copy(
                    src_ref=piece(br, c), dst_ref=piece(bc, c), send_sem=c_send.at[slot, c],
                    recv_sem=c_recv.at[c], device_id=to, device_id_type=pl.DeviceIdType.MESH,
                ).start()

    def take(c):
        remote(piece(br, c), b_send.at[0, c], b_recv.at[c], right).wait_recv()
        pass_on(piece(br, c), b_send, b_recv, c)
        give(c)

    def forward(c):
        @pl.when(relay)
        def _():
            remote(piece(bc, c), c_send.at[0, c], c_recv.at[c], far).wait_recv()
            remote(piece(bc, c), c_send.at[1, c], c_recv.at[c], near).start()

    give(column)
    between = {}
    between[1] = [functools.partial(at_distance, 1, take)]
    between[2] = [functools.partial(forward, column)]
    between[3] = [functools.partial(at_distance, 2, take)]
    between[4] = [functools.partial(at_distance, 1, forward)]
    between[5] = [functools.partial(at_distance, d, take) for d in range(3, columns)]
    between[6] = [functools.partial(at_distance, d, forward) for d in range(2, columns)]
    factor_in_place(a, w, between)
    for c in range(columns):
        @pl.when(from_near)
        def _(c=c):
            remote(piece(bc, c), c_send.at[0, c], c_recv.at[c], near).wait_recv()

        @pl.when(relay)
        def _(c=c):
            remote(piece(bc, c), c_send.at[1, c], c_recv.at[c], near).wait_send()

        @pl.when(root)
        def _(c=c):
            remote(piece(br, c), c_send.at[0, c], c_recv.at[c], far).wait_send()
            remote(piece(br, c), c_send.at[1, c], c_recv.at[c], near).wait_send()

        passed(piece(br, c), b_send, b_recv, c)

    @pl.when(root)
    def _():
        bc[...] = br[...]


def gather_factor_call(diag, lower, rows, columns):
    n = diag.shape[1]
    q = lower.shape[0] * columns
    dma = pltpu.SemaphoreType.DMA
    return pl.pallas_call(
        functools.partial(gather_factor_kernel, rows, columns),
        name="gather_factor",
        out_shape=(
            jax.ShapeDtypeStruct((n, n), F32),
            jax.ShapeDtypeStruct((n // BLOCK, BLOCK, BLOCK), F32),
            jax.ShapeDtypeStruct((q, n), F32),
            jax.ShapeDtypeStruct((q, n), F32),
        ),
        in_specs=[pl.BlockSpec(memory_space=pl.ANY)] * 2,
        out_specs=(VMEM,) * 4,
        scratch_shapes=[
            dma((2,)), dma((2, columns)), dma((columns,)), dma((columns,)), dma((columns,)),
            dma((2, columns)), dma((2, columns)), dma((2, columns)), dma((columns,)),
            dma((2, columns)), dma((columns,)),
        ],
        compiler_params=pltpu.CompilerParams(
            vmem_limit_bytes=40 << 20, collective_id=0, has_side_effects=True
        ),
    )(diag, lower)


def update_kernel(
    owners, slots, quarter, map_ref, l_ref, w_ref, br_ref, bc_ref, t_ref,
    panel_ref, out_ref, source_ref, xh, xl, lh, ll,
):
    n = l_ref.shape[0]
    q = br_ref.shape[0]
    share = panel_ref.shape[0]
    child = lax.axis_index("wide")
    row = lax.axis_index("grow")
    column = lax.axis_index("gcol")
    blocks = q // BLOCK
    per_owner = quarter // owners
    tile = 2 * BLOCK
    sides = (br_ref, bc_ref)
    lh[...], ll[...] = parts(l_ref[...])
    pair = 2 * BLOCK
    for k in range(n // pair):
        low, high = k * pair, k * pair + pair
        wa, wb = w_ref[2 * k], w_ref[2 * k + 1]
        across = l_ref[low + BLOCK : high, low : low + BLOCK]
        wk = parts(square(wa, -full_dot(wb, full_dot(across, wa, NN), NN), wb))

        def solve(i, carry, low=low, high=high, wk=wk):
            o = pl.multiple_of(i * tile, tile)
            for side, b in enumerate(sides):
                rest = b[pl.ds(o, tile), low:high]
                at = pl.ds(side * q + o, tile)
                if low:
                    rest = rest - split_dot(
                        (xh[at, :low], xl[at, :low]), (lh[low:high, :low], ll[low:high, :low]), NT
                    )
                x = split_dot(parts(rest), wk, NT)
                xh[at, low:high], xl[at, low:high] = parts(x)
                if side == 0:
                    br_ref[pl.ds(o, tile), low:high] = x
            return carry

        lax.fori_loop(0, q // tile, solve, 0)
    panel_ref[...] = br_ref[pl.ds(pl.multiple_of(column * share, share), share), :]

    def clear(i, carry):
        source_ref[i] = -1
        return carry

    lax.fori_loop(0, owners * per_owner, clear, 0)

    def place(g, carry):
        for b in range(blocks):
            to = map_ref[g, row * blocks + b] % quarter
            rank = jnp.int32(0)
            for e in range(b):
                other = map_ref[g, row * blocks + e] % quarter
                rank += (other // per_owner == to // per_owner).astype(jnp.int32)

            @pl.when(to // per_owner == child)
            def _(to=to, rank=rank):
                source_ref[g * per_owner + to % per_owner] = rank

        return carry

    lax.fori_loop(0, owners, place, 0)

    step = 3 if blocks % 3 == 0 else 1
    for first in range(0, blocks, step):
        low, high = first * BLOCK, (first + step) * BLOCK
        update = split_dot((xh[low:high, :], xl[low:high, :]), (xh[q:, :], xl[q:, :]), NT)
        for b in range(first, first + step):
            o = b * BLOCK
            to = (map_ref[child, row * blocks + b] % quarter) // per_owner
            rank = jnp.int32(0)
            for e in range(b):
                other = (map_ref[child, row * blocks + e] % quarter) // per_owner
                rank += (other == to).astype(jnp.int32)
            out_ref[to * slots + rank] = (
                t_ref[o : o + BLOCK, :] - update[o - low : o - low + BLOCK, :]
            )


def update_call(row_map, factor, inverses, b_row, b_col, trailing, share, owners, slots, quarter):
    n = factor.shape[0]
    q = b_row.shape[0]
    return pl.pallas_call(
        functools.partial(update_kernel, owners, slots, quarter),
        name="update",
        out_shape=(
            jax.ShapeDtypeStruct((share, n), F32),
            jax.ShapeDtypeStruct((owners * slots, BLOCK, q), F32),
            jax.ShapeDtypeStruct((quarter,), jnp.int32),
        ),
        in_specs=[SMEM] + [VMEM] * 5,
        out_specs=(VMEM, VMEM, SMEM),
        scratch_shapes=[
            pltpu.VMEM((2 * q, n), BF16),
            pltpu.VMEM((2 * q, n), BF16),
            pltpu.VMEM((n, n), BF16),
            pltpu.VMEM((n, n), BF16),
        ],
        compiler_params=pltpu.CompilerParams(vmem_limit_bytes=56 << 20),
    )(row_map, factor, inverses, b_row, b_col, trailing)


def add_kernel(owners, map_ref, source_ref, parent_ref, in_ref, out_ref):
    p, g = pl.program_id(0), pl.program_id(1)
    per_owner = pl.num_programs(0)
    blocks = in_ref.shape[2] // BLOCK
    column_blocks = out_ref.shape[2] // BLOCK
    column = lax.axis_index("gcol")

    @pl.when(g == 0)
    def _():
        out_ref[...] = parent_ref[...]

    @pl.when(source_ref[g * per_owner + p] >= 0)
    def _():
        for b in range(blocks):
            to = map_ref[g, column * blocks + b] % column_blocks
            at = pl.ds(pl.multiple_of(to * BLOCK, BLOCK), BLOCK)
            out_ref[0, :, at] += in_ref[0, :, b * BLOCK : b * BLOCK + BLOCK]


def add_call(row_map, source, parent, incoming, owners, slots):
    _, rows, width = parent.shape
    per_owner = rows // BLOCK

    def pick(p, g, map_ref, source_ref):
        return (g * slots + jnp.maximum(source_ref[g * per_owner + p], 0), 0, 0)

    block = pl.BlockSpec((1, BLOCK, width), lambda p, g, *_: (0, p, 0))
    return pl.pallas_call(
        functools.partial(add_kernel, owners),
        name="extend_add",
        out_shape=jax.ShapeDtypeStruct(parent.shape, F32),
        grid_spec=pltpu.PrefetchScalarGridSpec(
            num_scalar_prefetch=2,
            grid=(per_owner, owners),
            in_specs=[block, pl.BlockSpec((1, BLOCK, incoming.shape[2]), pick)],
            out_specs=block,
        ),
        compiler_params=pltpu.CompilerParams(vmem_limit_bytes=32 << 20),
    )(row_map, source, parent, incoming)


def body(diag_block, lower_block, trailing_block, parent_front, row_map):
    owners = lax.axis_size("wide")
    rows, columns = lax.axis_size("grow"), lax.axis_size("gcol")
    share = diag_block.shape[1]
    row, column = lax.axis_index("grow"), lax.axis_index("gcol")
    factor, inverses, b_row, b_col = gather_factor_call(
        diag_block[0], lower_block[0], rows, columns
    )
    factor_rows = lax.dynamic_slice_in_dim(factor, (row * columns + column) * share, share, 0)
    quarter = parent_front.shape[1] * owners // BLOCK
    blocks = trailing_block.shape[1] // BLOCK
    slots = min(blocks, quarter // owners)
    panel, outgoing, source = update_call(
        row_map, factor, inverses, b_row, b_col, trailing_block[0],
        lower_block.shape[1], owners, slots, quarter,
    )
    incoming = lax.all_to_all(outgoing, "wide", split_axis=0, concat_axis=0, tiled=True)
    parent = add_call(row_map, source, parent_front, incoming, owners, slots)
    return (factor_rows[None], panel[None], parent)


def solution(mesh):
    placed = (
        P("wide", ("grow", "gcol"), None),
        P("wide", ("grow", "gcol"), None),
        P("wide", "grow", "gcol"),
        P("grow", "wide", "gcol"),
        P(),
    )
    return jax.shard_map(
        body,
        mesh=mesh,
        in_specs=placed,
        out_specs=(
            P("wide", ("grow", "gcol"), None),
            P("wide", ("grow", "gcol"), None),
            P("grow", "wide", "gcol"),
        ),
        check_vma=False,
    )
```

profile of v0, /device:TPU:4, one launch (start us, length us, event | category | flops | bytes accessed | tf_op | source)
XLA Modules:
  0.0 207.7 jit_solution(1960702490066942595)
XLA Ops:
  0.6 0.0 copy-start.4
  0.6 1.1 copy-done.4
  1.8 0.0 copy-start.6
  1.8 0.9 copy-done.6
  2.7 96.9 %gather_factor.1 = (f32[1024,1024]{1,0:T(8,128)S(1)}, f32[8,128,128]{2,1,0:T(8,128)S(1)}, f32[768,1024]{1,0:T(8,128)S(1)}, f32[768,1024]{1,0:T(8,128)S(1)}) custom-call(f32[64,1024]{1,0:T(8,128)S(1)} %bitcast.7, f32[192,1024]{1,0:T(8,128)S(1)} %bitcast.6), custom_call_target="tpu_custom_call" | custom-call | tf_op jit(solution)/shard_map/gather_factor/pallas_call | solution.py:272
  99.6 0.0 copy-start.1
  99.6 1.9 copy-done.1
  101.6 0.0 copy-start.2
  101.6 1.7 copy-done.2
  103.3 0.0 copy-start.3
  103.3 1.7 copy-done.3
  105.0 0.0 copy-start.5
  105.0 0.8 copy-done.5
  105.8 30.0 %update.1 = (f32[192,1024]{1,0:T(8,128)}, f32[12,128,768]{2,1,0:T(8,128)}, s32[16]{0:T(128)}) custom-call(s32[2,24]{1,0:T(2,128)} %map_ref.3, f32[1024,1024]{1,0:T(8,128)} %copy-done.1, f32[8,128,128]{2,1,0:T(8,128)} %copy-done.5, f32[768,1024]{1,0:T(8,128)} %copy-done.2, f32[768,1024]{1,0:T(8,128)} %copy-done.3, f32[768,768]{1,0:T(8,128)} %bitcast.8), custom_call_target="tpu_custom_call" | custom-call | tf_op jit(solution)/shard_map/update/pallas_call | solution.py:375
  135.8 0.0 copy-start.7
  135.8 0.0 copy-start.8
  135.8 5.8 %all-to-all-start = ((f32[12,128,768]{2,1,0:T(8,128)}), f32[12,128,768]{2,1,0:T(8,128)}, u32[]{:S(2)}, u32[]{:S(2)}) async-start(f32[12,128,768]{2,1,0:T(8,128)} %get-tuple-element.16), calls=%async_computation | async-start | bytes 9437184 | tf_op jit(solution)/shard_map/all_to_all | solution.py:452
  141.6 1.7 dynamic-slice_bitcast_fusion
  143.3 49.1 %all-to-all-done.in_ref = f32[12,128,768]{2,1,0:T(8,128)} async-done(((f32[12,128,768]{2,1,0:T(8,128)}), f32[12,128,768]{2,1,0:T(8,128)}, u32[]{:S(2)}, u32[]{:S(2)}) %all-to-all-start) | async-done | bytes 4718624 | tf_op jit(solution)/shard_map/all_to_all | solution.py:452
  192.4 0.0 copy-done.7
  192.4 0.0 copy-done.8
  192.4 0.0 copy-start
  192.4 3.4 %copy-done = f32[1,1024,2048]{2,1,0:T(8,128)S(1)} copy-done((f32[1,1024,2048]{2,1,0:T(8,128)S(1)}, f32[1,1024,2048]{2,1,0:T(8,128)}, u32[]{:S(2)}) %copy-start) | copy-done | bytes 8388632
  195.8 12.0 %extend_add.1 = f32[1,1024,2048]{2,1,0:T(8,128)} custom-call(s32[2,24]{1,0:T(2,128)S(1)} %copy-done.7, s32[16]{0:T(128)S(1)} %copy-done.8, f32[1,1024,2048]{2,1,0:T(8,128)S(1)} %copy-done, f32[12,128,768]{2,1,0:T(8,128)} %all-to-all-done.in_ref), custom_call_target="tpu_custom_call" | custom-call | tf_op jit(solution)/shard_map/extend_add/pallas_call | solution.py:422
Async XLA Ops:
  0.6 1.1 copy-start.4
  1.8 0.9 copy-start.6
  99.6 2.0 copy-start.1
  101.6 1.7 copy-start.2
  103.3 1.7 copy-start.3
  105.0 0.8 copy-start.5
  135.8 56.6 %copy-start.7 = (s32[2,24]{1,0:T(2,128)S(1)}, s32[2,24]{1,0:T(2,128)}, u32[]{:S(2)}) copy-start(s32[2,24]{1,0:T(2,128)} %map_ref.3) | copy-start | bytes 580
  135.8 56.6 %copy-start.8 = (s32[16]{0:T(128)S(1)}, s32[16]{0:T(128)}, u32[]{:S(2)}) copy-start(s32[16]{0:T(128)} %get-tuple-element.15.source_ref) | copy-start | bytes 196
  135.8 56.6 %all-to-all-start = ((f32[12,128,768]{2,1,0:T(8,128)}), f32[12,128,768]{2,1,0:T(8,128)}, u32[]{:S(2)}, u32[]{:S(2)}) async-start(f32[12,128,768]{2,1,0:T(8,128)} %get-tuple-element.16), calls=%async_computation | async-start | bytes 9437184 | tf_op jit(solution)/shard_map/all_to_all | solution.py:452
  192.4 3.4 %copy-start = (f32[1,1024,2048]{2,1,0:T(8,128)S(1)}, f32[1,1024,2048]{2,1,0:T(8,128)}, u32[]{:S(2)}) copy-start(f32[1,1024,2048]{2,1,0:T(8,128)} %parent_ref.1) | copy-start | bytes 25165828
where the time goes:
time: 208 us
  Pallas kernels  139 us (67%)
  waiting for transfers between devices  49.1 us (24%)
  local copies, waits for them, and re-layouts  13.3 us (6%)
  starting transfers between devices  5.81 us (3%)
    pallas_call x1, Pallas kernels, gather_factor_call(): pl.pallas_call(functools.partial(gather_factor_kernel, rows, columns), na...  96.9 us
    all_to_all x1, waiting for transfers between devices, body(): lax.all_to_all(outgoing, 'wide', split_axis=0, concat_axis=0, tiled=True)  49.1 us
    pallas_call x1, Pallas kernels, update_call(): pl.pallas_call(functools.partial(update_kernel, owners, slots, quarter),...  30 us
    pallas_call x1, Pallas kernels, add_call(): pl.pallas_call(functools.partial(add_kernel, owners), name='extend_add',...  12 us
    unnamed x18, local copies, waits for them, and re-layouts  11.6 us
    all_to_all x1, starting transfers between devices, body(): lax.all_to_all(outgoing, 'wide', split_axis=0, concat_axis=0, tiled=True)  5.81 us
  transfers between devices with their start and end apart: 1, of which 1 were waited for; matrix products, arithmetic and copies ran while one was open for 1% of the time, Pallas kernels for 0%

commit v1 on v0

--- a/solution.py
+++ b/solution.py
@@ -117,12 +117,54 @@
     lax.fori_loop(0, count, step, 0)
 
 
-def gather_factor_kernel(
-    rows, columns, d_ref, x_ref, a, w, br, bc,
+def most_slots(blocks, per_owner):
+    return min(blocks, per_owner)
+
+
+def solve_sides(l_ref, w_ref, br_ref, bc_ref, xh, xl, lh, ll):
+    n = l_ref.shape[0]
+    blocks = br_ref.shape[0] // BLOCK
+    few = 2
+    tile = few * BLOCK
+    sides = (br_ref, bc_ref)
+    lh[...], ll[...] = parts(l_ref[...])
+    pair = 2 * BLOCK
+    for k in range(n // pair):
+        low, high = k * pair, k * pair + pair
+        wa, wb = w_ref[2 * k], w_ref[2 * k + 1]
+        across = l_ref[low + BLOCK : high, low : low + BLOCK]
+        wk = parts(square(wa, -full_dot(wb, full_dot(across, wa, NN), NN), wb))
+
+        def solve(i, carry, low=low, high=high, wk=wk):
+            o = pl.multiple_of(i * tile, tile)
+            for side, b in enumerate(sides):
+                rest = b[pl.ds(o, tile), low:high]
+                at = pl.ds(side * blocks + i * few, few)
+                if low:
+                    left = tuple(x[at, :, :low].reshape(tile, low) for x in (xh, xl))
+                    rest = rest - split_dot(left, (lh[low:high, :low], ll[low:high, :low]), NT)
+                x = split_dot(parts(rest), wk, NT)
+                for ref, value in zip((xh, xl), parts(x)):
+                    ref[at, :, low:high] = value.reshape(few, BLOCK, pair)
+                if side == 0:
+                    br_ref[pl.ds(o, tile), low:high] = x
+            return carry
+
+        lax.fori_loop(0, blocks // few, solve, 0)
+
+
+def front_kernel(
+    rows, columns, owners, sure, quarter, map_ref, d_ref, x_ref, t_ref,
+    factor_ref, panel_ref, piece_ref, need_ref,
+    a, w, br, bc, xh, xl, lh, ll, t, stage, x_send, x_recv,
     local, line_send, line_recv, far_send, far_recv, near_send, near_recv,
     b_send, b_recv, c_send, c_recv,
 ):
+    child = lax.axis_index("wide")
     row, column = lax.axis_index("grow"), lax.axis_index("gcol")
+    q = br.shape[0]
+    blocks = q // BLOCK
+    per_owner = quarter // owners
     far_row = lax.rem(row + rows // 2, rows)
     near_row = row + 1 - 2 * lax.rem(row, 2)
     right, left = {"gcol": column + 1}, {"gcol": column - 1}
@@ -144,14 +186,21 @@
 
     own_d = pltpu.make_async_copy(d_ref, band(row, column), local.at[0])
     own_x = pltpu.make_async_copy(x_ref, piece(br, column), local.at[1])
+    own_t = pltpu.make_async_copy(t_ref, t, local.at[2])
     own_d.start()
     own_x.start()
+    own_t.start()
     barrier = pltpu.get_barrier_semaphore()
     next_column = {"gcol": lax.rem(column + 1, columns)}
     last_column = {"gcol": lax.rem(column + columns - 1, columns)}
     for to in (far, near, next_column, last_column):
         pl.semaphore_signal(barrier, inc=1, device_id=to, device_id_type=pl.DeviceIdType.MESH)
-    pl.semaphore_wait(barrier, 4)
+    for d in range(1, owners):
+        pl.semaphore_signal(
+            barrier, inc=1, device_id={"wide": lax.rem(child + d, owners)},
+            device_id_type=pl.DeviceIdType.MESH,
+        )
+    pl.semaphore_wait(barrier, 3 + owners)
     own_d.wait()
     own_x.wait()
 
@@ -245,6 +294,7 @@
     between[6] = [functools.partial(at_distance, d, forward) for d in range(2, columns)]
     factor_in_place(a, w, between)
     for c in range(columns):
+
         @pl.when(from_near)
         def _(c=c):
             remote(piece(bc, c), c_send.at[0, c], c_recv.at[c], near).wait_recv()
@@ -265,193 +315,231 @@
         bc[...] = br[...]
 
 
-def gather_factor_call(diag, lower, rows, columns):
+    factor_ref[...] = a[pl.ds(pl.multiple_of((row * columns + column) * share, share), share), :]
+    solve_sides(a, w, br, bc, xh, xl, lh, ll)
+    own_t.wait()
+
+    def owner(g, r, b):
+        return (map_ref[g, r * blocks + b] % quarter) // per_owner
+
+    mine = [owner(child, row, b) for b in range(blocks)]
+
+    def pick(to, slot):
+        block, rank = jnp.int32(0), jnp.int32(0)
+        for b in range(blocks):
+            here = mine[b] == to
+            block = jnp.where(here & (rank == slot), b, block)
+            rank += here.astype(jnp.int32)
+        return block
+
+    def give_away(s, d):
+        return pltpu.make_async_remote_copy(
+            src_ref=stage.at[s], dst_ref=piece_ref.at[blocks + s],
+            send_sem=x_send.at[s], recv_sem=x_recv.at[s],
+            device_id={"wide": lax.rem(child + d, owners)}, device_id_type=pl.DeviceIdType.MESH,
+        )
+
+    slots = [(d, i) for d in range(1, owners) for i in range(sure)]
+    columns_side = tuple(x[blocks:].reshape(q, x.shape[2]) for x in (xh, xl))
+    for first in range(0, len(slots), 2):
+        group = slots[first : first + 2]
+        at = [pick(lax.rem(child + d, owners), i) for d, i in group]
+        sides = tuple(jnp.concatenate([x[p] for p in at], axis=0) for x in (xh, xl))
+        product = split_dot(sides, columns_side, NT)
+        for n, (p, (d, _)) in enumerate(zip(at, group)):
+            stage[first + n] = t[p] - product[n * BLOCK : n * BLOCK + BLOCK, :]
+            give_away(first + n, d).start()
+    panel_ref[...] = br[pl.ds(pl.multiple_of(column * part, part), part), :]
+    step = 3 if blocks % 3 == 0 else 1
+    for first in range(0, blocks, step):
+        low, high = first * BLOCK, (first + step) * BLOCK
+        rows_side = tuple(x[first : first + step].reshape(high - low, x.shape[2]) for x in (xh, xl))
+        product = split_dot(rows_side, columns_side, NT)
+        for b in range(first, first + step):
+            o = b * BLOCK
+            piece_ref[b] = t[b] - product[o - low : o - low + BLOCK, :]
+    need = jnp.int32(0)
+    if sure < most_slots(blocks, per_owner):
+        for g in range(owners):
+            for r in range(rows):
+                there = [owner(g, r, b) for b in range(blocks)]
+                for e in range(owners):
+                    if e != g:
+                        need = jnp.maximum(need, sum((x == e).astype(jnp.int32) for x in there))
+    need_ref[0] = need
+    for s, (d, _) in enumerate(slots):
+        give_away(s, d).wait()
+
+
+def front_call(row_map, diag, lower, trailing, rows, columns, owners, sure, quarter):
     n = diag.shape[1]
-    q = lower.shape[0] * columns
+    share, part = diag.shape[0], lower.shape[0]
+    q = part * columns
+    blocks = q // BLOCK
     dma = pltpu.SemaphoreType.DMA
+    away = (owners - 1) * sure
     return pl.pallas_call(
-        functools.partial(gather_factor_kernel, rows, columns),
-        name="gather_factor",
+        functools.partial(front_kernel, rows, columns, owners, sure, quarter),
+        name="front",
         out_shape=(
-            jax.ShapeDtypeStruct((n, n), F32),
-            jax.ShapeDtypeStruct((n // BLOCK, BLOCK, BLOCK), F32),
-            jax.ShapeDtypeStruct((q, n), F32),
-            jax.ShapeDtypeStruct((q, n), F32),
+            jax.ShapeDtypeStruct((share, n), F32),
+            jax.ShapeDtypeStruct((part, n), F32),
+            jax.ShapeDtypeStruct((blocks + away, BLOCK, q), F32),
+            jax.ShapeDtypeStruct((1,), jnp.int32),
         ),
-        in_specs=[pl.BlockSpec(memory_space=pl.ANY)] * 2,
-        out_specs=(VMEM,) * 4,
+        in_specs=[SMEM] + [pl.BlockSpec(memory_space=pl.ANY)] * 3,
+        out_specs=(VMEM,) * 3 + (SMEM,),
         scratch_shapes=[
-            dma((2,)), dma((2, columns)), dma((columns,)), dma((columns,)), dma((columns,)),
+            pltpu.VMEM((n, n), F32),
+            pltpu.VMEM((n // BLOCK, BLOCK, BLOCK), F32),
+            pltpu.VMEM((q, n), F32),
+            pltpu.VMEM((q, n), F32),
+            pltpu.VMEM((2 * blocks, BLOCK, n), BF16),
+            pltpu.VMEM((2 * blocks, BLOCK, n), BF16),
+            pltpu.VMEM((n, n), BF16),
+            pltpu.VMEM((n, n), BF16),
+            pltpu.VMEM((blocks, BLOCK, q), F32),
+            pltpu.VMEM((away, BLOCK, q), F32),
+            dma((away,)), dma((away,)),
+            dma((3,)), dma((2, columns)), dma((columns,)), dma((columns,)), dma((columns,)),
             dma((2, columns)), dma((2, columns)), dma((2, columns)), dma((columns,)),
             dma((2, columns)), dma((columns,)),
         ],
         compiler_params=pltpu.CompilerParams(
-            vmem_limit_bytes=40 << 20, collective_id=0, has_side_effects=True
+            vmem_limit_bytes=56 << 20, collective_id=0, has_side_effects=True
         ),
-    )(diag, lower)
-
-
-def update_kernel(
-    owners, slots, quarter, map_ref, l_ref, w_ref, br_ref, bc_ref, t_ref,
-    panel_ref, out_ref, source_ref, xh, xl, lh, ll,
-):
-    n = l_ref.shape[0]
-    q = br_ref.shape[0]
-    share = panel_ref.shape[0]
-    child = lax.axis_index("wide")
-    row = lax.axis_index("grow")
+    )(row_map, diag, lower, trailing.reshape(blocks, BLOCK, q))
+
+
+def rest_kernel(owners, sure, more, quarter, map_ref, piece_ref, out_ref, stage, send, recv):
+    child, row = lax.axis_index("wide"), lax.axis_index("grow")
+    blocks = out_ref.shape[2] // BLOCK
+    per_owner = quarter // owners
+    barrier = pltpu.get_barrier_semaphore()
+    for d in range(1, owners):
+        pl.semaphore_signal(
+            barrier, inc=1, device_id={"wide": lax.rem(child + d, owners)},
+            device_id_type=pl.DeviceIdType.MESH,
+        )
+    mine = [(map_ref[child, row * blocks + b] % quarter) // per_owner for b in range(blocks)]
+
+    def give_away(s, d):
+        return pltpu.make_async_remote_copy(
+            src_ref=stage.at[s], dst_ref=out_ref.at[s], send_sem=send.at[s], recv_sem=recv.at[s],
+            device_id={"wide": lax.rem(child + d, owners)}, device_id_type=pl.DeviceIdType.MESH,
+        )
+
+    slots = [(d, sure + i) for d in range(1, owners) for i in range(more)]
+    for s, (d, slot) in enumerate(slots):
+        block, rank = jnp.int32(0), jnp.int32(0)
+        for b in range(blocks):
+            here = mine[b] == lax.rem(child + d, owners)
+            block = jnp.where(here & (rank == slot), b, block)
+            rank += here.astype(jnp.int32)
+        stage[s] = piece_ref[block]
+    pl.semaphore_wait(barrier, owners - 1)
+    for s, (d, _) in enumerate(slots):
+        give_away(s, d).start()
+    for s, (d, _) in enumerate(slots):
+        give_away(s, d).wait()
+
+
+def rest_call(row_map, pieces, owners, sure, more, quarter):
+    away = (owners - 1) * more
+    shape = (away,) + pieces.shape[1:]
+    dma = pltpu.SemaphoreType.DMA
+    return pl.pallas_call(
+        functools.partial(rest_kernel, owners, sure, more, quarter),
+        name="rest",
+        out_shape=jax.ShapeDtypeStruct(shape, F32),
+        in_specs=[SMEM, VMEM],
+        out_specs=VMEM,
+        scratch_shapes=[pltpu.VMEM(shape, F32), dma((away,)), dma((away,))],
+        compiler_params=pltpu.CompilerParams(
+            vmem_limit_bytes=12 << 20, collective_id=1, has_side_effects=True
+        ),
+    )(row_map, pieces)
+
+
+def add_kernel(owners, sure, map_ref, parent_ref, *refs):
+    pieces, out_ref = refs[:-1], refs[-1]
+    p = pl.program_id(0)
+    per_owner = pl.num_programs(0)
+    quarter = owners * per_owner
+    q = pieces[0].shape[2]
+    blocks = q // BLOCK
+    column_blocks = out_ref.shape[2] // BLOCK
+    child, row = lax.axis_index("wide"), lax.axis_index("grow")
     column = lax.axis_index("gcol")
-    blocks = q // BLOCK
-    per_owner = quarter // owners
-    tile = 2 * BLOCK
-    sides = (br_ref, bc_ref)
-    lh[...], ll[...] = parts(l_ref[...])
-    pair = 2 * BLOCK
-    for k in range(n // pair):
-        low, high = k * pair, k * pair + pair
-        wa, wb = w_ref[2 * k], w_ref[2 * k + 1]
-        across = l_ref[low + BLOCK : high, low : low + BLOCK]
-        wk = parts(square(wa, -full_dot(wb, full_dot(across, wa, NN), NN), wb))
-
-        def solve(i, carry, low=low, high=high, wk=wk):
-            o = pl.multiple_of(i * tile, tile)
-            for side, b in enumerate(sides):
-                rest = b[pl.ds(o, tile), low:high]
-                at = pl.ds(side * q + o, tile)
-                if low:
-                    rest = rest - split_dot(
-                        (xh[at, :low], xl[at, :low]), (lh[low:high, :low], ll[low:high, :low]), NT
-                    )
-                x = split_dot(parts(rest), wk, NT)
-                xh[at, low:high], xl[at, low:high] = parts(x)
-                if side == 0:
-                    br_ref[pl.ds(o, tile), low:high] = x
-            return carry
-
-        lax.fori_loop(0, q // tile, solve, 0)
-    panel_ref[...] = br_ref[pl.ds(pl.multiple_of(column * share, share), share), :]
-
-    def clear(i, carry):
-        source_ref[i] = -1
-        return carry
-
-    lax.fori_loop(0, owners * per_owner, clear, 0)
-
-    def place(g, carry):
+    out_ref[...] = parent_ref[...]
+
+    def add(g, carry):
+        block, slot, rank = jnp.int32(-1), jnp.int32(-1), jnp.int32(0)
         for b in range(blocks):
             to = map_ref[g, row * blocks + b] % quarter
-            rank = jnp.int32(0)
-            for e in range(b):
-                other = map_ref[g, row * blocks + e] % quarter
-                rank += (other // per_owner == to // per_owner).astype(jnp.int32)
-
-            @pl.when(to // per_owner == child)
-            def _(to=to, rank=rank):
-                source_ref[g * per_owner + to % per_owner] = rank
+            hit = to == child * per_owner + p
+            block = jnp.where(hit, b, block)
+            slot = jnp.where(hit, rank, slot)
+            rank += (to // per_owner == child).astype(jnp.int32)
+        away = lax.rem(child - g + owners, owners) - 1
+
+        def put(ref, index):
+            for b in range(blocks):
+                to = map_ref[g, column * blocks + b] % column_blocks
+                at = pl.ds(pl.multiple_of(to * BLOCK, BLOCK), BLOCK)
+                out_ref[0, :, at] += ref[index, :, b * BLOCK : b * BLOCK + BLOCK]
+
+        more = most_slots(blocks, per_owner) - sure
+
+        @pl.when((block >= 0) & ((g == child) | (slot < sure)))
+        def _():
+            put(pieces[0], jnp.where(g == child, block, blocks + away * sure + slot))
+
+        if len(pieces) > 1:
+
+            @pl.when((block >= 0) & (g != child) & (slot >= sure))
+            def _():
+                put(pieces[1], away * more + slot - sure)
 
         return carry
 
-    lax.fori_loop(0, owners, place, 0)
-
-    step = 3 if blocks % 3 == 0 else 1
-    for first in range(0, blocks, step):
-        low, high = first * BLOCK, (first + step) * BLOCK
-        update = split_dot((xh[low:high, :], xl[low:high, :]), (xh[q:, :], xl[q:, :]), NT)
-        for b in range(first, first + step):
-            o = b * BLOCK
-            to = (map_ref[child, row * blocks + b] % quarter) // per_owner
-            rank = jnp.int32(0)
-            for e in range(b):
-                other = (map_ref[child, row * blocks + e] % quarter) // per_owner
-                rank += (other == to).astype(jnp.int32)
-            out_ref[to * slots + rank] = (
-                t_ref[o : o + BLOCK, :] - update[o - low : o - low + BLOCK, :]
-            )
-
-
-def update_call(row_map, factor, inverses, b_row, b_col, trailing, share, owners, slots, quarter):
-    n = factor.shape[0]
-    q = b_row.shape[0]
+    lax.fori_loop(0, owners, add, 0)
+
+
+def add_call(row_map, parent, pieces, owners, sure):
+    _, rows, width = parent.shape
+    block = pl.BlockSpec((1, BLOCK, width), lambda p: (0, p, 0))
     return pl.pallas_call(
-        functools.partial(update_kernel, owners, slots, quarter),
-        name="update",
-        out_shape=(
-            jax.ShapeDtypeStruct((share, n), F32),
-            jax.ShapeDtypeStruct((owners * slots, BLOCK, q), F32),
-            jax.ShapeDtypeStruct((quarter,), jnp.int32),
-        ),
-        in_specs=[SMEM] + [VMEM] * 5,
-        out_specs=(VMEM, VMEM, SMEM),
-        scratch_shapes=[
-            pltpu.VMEM((2 * q, n), BF16),
-            pltpu.VMEM((2 * q, n), BF16),
-            pltpu.VMEM((n, n), BF16),
-            pltpu.VMEM((n, n), BF16),
-        ],
-        compiler_params=pltpu.CompilerParams(vmem_limit_bytes=56 << 20),
-    )(row_map, factor, inverses, b_row, b_col, trailing)
-
-
-def add_kernel(owners, map_ref, source_ref, parent_ref, in_ref, out_ref):
-    p, g = pl.program_id(0), pl.program_id(1)
-    per_owner = pl.num_programs(0)
-    blocks = in_ref.shape[2] // BLOCK
-    column_blocks = out_ref.shape[2] // BLOCK
-    column = lax.axis_index("gcol")
-
-    @pl.when(g == 0)
-    def _():
-        out_ref[...] = parent_ref[...]
-
-    @pl.when(source_ref[g * per_owner + p] >= 0)
-    def _():
-        for b in range(blocks):
-            to = map_ref[g, column * blocks + b] % column_blocks
-            at = pl.ds(pl.multiple_of(to * BLOCK, BLOCK), BLOCK)
-            out_ref[0, :, at] += in_ref[0, :, b * BLOCK : b * BLOCK + BLOCK]
-
-
-def add_call(row_map, source, parent, incoming, owners, slots):
-    _, rows, width = parent.shape
-    per_owner = rows // BLOCK
-
-    def pick(p, g, map_ref, source_ref):
-        return (g * slots + jnp.maximum(source_ref[g * per_owner + p], 0), 0, 0)
-
-    block = pl.BlockSpec((1, BLOCK, width), lambda p, g, *_: (0, p, 0))
-    return pl.pallas_call(
-        functools.partial(add_kernel, owners),
+        functools.partial(add_kernel, owners, sure),
         name="extend_add",
         out_shape=jax.ShapeDtypeStruct(parent.shape, F32),
-        grid_spec=pltpu.PrefetchScalarGridSpec(
-            num_scalar_prefetch=2,
-            grid=(per_owner, owners),
-            in_specs=[block, pl.BlockSpec((1, BLOCK, incoming.shape[2]), pick)],
-            out_specs=block,
-        ),
-        compiler_params=pltpu.CompilerParams(vmem_limit_bytes=32 << 20),
-    )(row_map, source, parent, incoming)
+        grid=(rows // BLOCK,),
+        in_specs=[SMEM, block] + [VMEM] * len(pieces),
+        out_specs=block,
+        compiler_params=pltpu.CompilerParams(vmem_limit_bytes=20 << 20),
+    )(row_map, parent, *pieces)
 
 
 def body(diag_block, lower_block, trailing_block, parent_front, row_map):
     owners = lax.axis_size("wide")
     rows, columns = lax.axis_size("grow"), lax.axis_size("gcol")
-    share = diag_block.shape[1]
-    row, column = lax.axis_index("grow"), lax.axis_index("gcol")
-    factor, inverses, b_row, b_col = gather_factor_call(
-        diag_block[0], lower_block[0], rows, columns
-    )
-    factor_rows = lax.dynamic_slice_in_dim(factor, (row * columns + column) * share, share, 0)
     quarter = parent_front.shape[1] * owners // BLOCK
     blocks = trailing_block.shape[1] // BLOCK
-    slots = min(blocks, quarter // owners)
-    panel, outgoing, source = update_call(
-        row_map, factor, inverses, b_row, b_col, trailing_block[0],
-        lower_block.shape[1], owners, slots, quarter,
+    most = most_slots(blocks, quarter // owners)
+    sure = max(1, 2 * most // 3)
+    factor, panel, pieces, need = front_call(
+        row_map, diag_block[0], lower_block[0], trailing_block[0], rows, columns, owners, sure, quarter,
     )
-    incoming = lax.all_to_all(outgoing, "wide", split_axis=0, concat_axis=0, tiled=True)
-    parent = add_call(row_map, source, parent_front, incoming, owners, slots)
-    return (factor_rows[None], panel[None], parent)
+
+    def few():
+        return add_call(row_map, parent_front, (pieces,), owners, sure)
+
+    def many():
+        rest = rest_call(row_map, pieces, owners, sure, most - sure, quarter)
+        return add_call(row_map, parent_front, (pieces, rest), owners, sure)
+
+    parent = lax.cond(need[0] > sure, many, few) if most > sure else few()
+    return (factor[None], panel[None], parent)
 
 
 def solution(mesh):

time: 208 us -> 163 us (0.78)
  waiting for transfers between devices: 49.1 us -> 0 us
  Pallas kernels: 139 us -> 160 us
  local copies, waits for them, and re-layouts: 13.3 us -> 1.59 us
  starting transfers between devices: 5.81 us -> 0 us
    all_to_all x1 -> x0, waiting for transfers between devices: 49.1 us -> none  [body(): lax.all_to_all(outgoing, 'wide', split_axis=0, concat_axis=0, tiled=True)]
    pallas_call x3 -> x2, Pallas kernels: 139 us -> 160 us  [the longest x1 150 us: front_call(): pl.pallas_call(functools.partial(front_kernel, rows, columns, owners, sur...]
    unnamed x18 -> x6, local copies, waits for them, and re-layouts: 11.6 us -> 1.59 us
    all_to_all x1 -> x0, starting transfers between devices: 5.81 us -> none  [body(): lax.all_to_all(outgoing, 'wide', split_axis=0, concat_axis=0, tiled=True)]
  transfers between devices with their start and end apart: 1 -> 0, of which waited for: 1 -> 0; matrix products, arithmetic and copies ran while one was open for 1% -> 0% of each run, Pallas kernels for 0% -> 0%
where the time goes in v1:
time: 163 us
  Pallas kernels  160 us (98%)
    pallas_call x1, Pallas kernels, front_call(): pl.pallas_call(functools.partial(front_kernel, rows, columns, owners, sur...  150 us
    pallas_call x1, Pallas kernels, add_call(): pl.pallas_call(functools.partial(add_kernel, owners, sure), name='extend_...  9.9 us

profile of v1, /device:TPU:4, one launch (start us, length us, event | category | flops | bytes accessed | tf_op | source)
XLA Modules:
  0.0 163.0 jit_solution(4730543721698582675)
XLA Ops:
  0.6 150.2 %front.1 = (f32[64,1024]{1,0:T(8,128)}, f32[192,1024]{1,0:T(8,128)}, f32[10,128,768]{2,1,0:T(8,128)S(1)}, s32[1]{0:T(128)}) custom-call(s32[2,24]{1,0:T(2,128)} %map_ref.1, f32[64,1024]{1,0:T(8,128)} %bitcast.9, f32[192,1024]{1,0:T(8,128)} %bitcast.8, f32[6,128,768]{2,1,0:T(8,128)} %bitcast.6), custom_call_target="tpu_custom_call" | custom-call | tf_op jit(solution)/shard_map/front/pallas_call | solution.py:381
  151.5 0.0 copy-start.1
  151.5 0.0 copy-start
  151.5 9.9 %conditional.1 = (f32[1,1024,2048]{2,1,0:T(8,128)}) conditional(s32[]{:T(128)} %bitcast.5, (s32[2,24]{1,0:T(2,128)}, f32[1,1024,2048]{2,1,0:T(8,128)}, f32[10,128,768]{2,1,0:T(8,128)S(1)}) %tuple.14, (s32[2,24]{1,0:T(2,128)}, f32[10,128,768]{2,1,0:T(8,128)S(1)}, f32[1,1024,2048]{2,1,0:T(8,128)}) %tuple.15), branch_computations={%region_0.0_spmd, %region_1.0_spmd} | conditional | bytes 8 | solution.py:541
  151.5 9.9 %extend_add.2 = f32[1,1024,2048]{2,1,0:T(8,128)} custom-call(s32[2,24]{1,0:T(2,128)} %get-tuple-element.8.map_ref, f32[1,1024,2048]{2,1,0:T(8,128)} %get-tuple-element.16.parent_ref, f32[10,128,768]{2,1,0:T(8,128)S(1)} %get-tuple-element.17.refs_0_), custom_call_target="tpu_custom_call" | custom-call | tf_op jit(solution)/shard_map/cond/branch_0_fun/extend_add/pallas_call | solution.py:512
  161.4 0.0 copy-done.1
  161.4 0.7 copy.12
  162.1 0.0 copy-done
  162.1 0.9 copy.13
Async XLA Ops:
  151.5 9.9 %copy-start.1 = (f32[64,1024]{1,0:T(8,128)S(1)}, f32[64,1024]{1,0:T(8,128)}, u32[]{:S(2)}) copy-start(f32[64,1024]{1,0:T(8,128)} %get-tuple-element.28) | copy-start | bytes 786436
  151.5 10.6 %copy-start = (f32[192,1024]{1,0:T(8,128)S(1)}, f32[192,1024]{1,0:T(8,128)}, u32[]{:S(2)}) copy-start(f32[192,1024]{1,0:T(8,128)} %get-tuple-element.29) | copy-start | bytes 2359300

commit v2 on v1

--- a/solution.py
+++ b/solution.py
@@ -1,4 +1,5 @@
 import functools
+import math
 
 import jax
 import jax.numpy as jnp
@@ -43,16 +44,18 @@
     wide = (8, 2 * half)
     groups = [full[8 * s : 8 * s + 8] for s in range(count)]
     sub = lax.broadcasted_iota(jnp.int32, wide, 0)
+    at_row = [jnp.full(wide, i, jnp.int32) for i in range(8)]
+    spread = lambda x: jnp.broadcast_to(x, wide)
+    take = lambda x, i: jnp.take_along_axis(x, at_row[i], axis=0, mode="promise_in_bounds")
     done = []
     for s in range(count):
         c = 8 * s
-        spread = lambda x: jnp.broadcast_to(x, wide)
+        column = {
+            t: [spread(groups[t][:, c + j : c + j + 1]) for j in range(8)] for t in range(s, count)
+        }
         lead = [spread(groups[s][i : i + 1, :]) for i in range(8)]
-        pivot = {
-            (i, j): spread(lead[i][:, c + j : c + j + 1]) for i in range(8) for j in range(i, 8)
-        }
+        pivot = {(i, j): take(column[s][j], i) for i in range(8) for j in range(i, 8)}
         below = range(s + 1, count)
-        column = {t: [spread(groups[t][:, c + j : c + j + 1]) for j in range(8)] for t in below}
         keep = jnp.zeros(wide, F32)
         for j in range(8):
             r = lax.rsqrt(pivot[j, j])
@@ -104,11 +107,15 @@
             def _(at=at):
                 low, high = at * BLOCK, at * BLOCK + BLOCK
                 a[low:high, high:] = jnp.zeros((BLOCK, n - high), F32)
-                p = full_dot(a[high:, low:high], w[at], NT)
+                p = split_dot(parts(a[high:, low:high]), parts(w[at]), NT)
                 a[high:, low:high] = p
+                ph, pl_ = parts(p)
                 for c in range(high, n, 2 * BLOCK):
                     e = min(c + 2 * BLOCK, n)
-                    a[c:, c:e] = a[c:, c:e] - full_dot(p[c - high :], p[c - high : e - high], NT)
+                    left, right = slice(c - high, None), slice(c - high, e - high)
+                    a[c:, c:e] = a[c:, c:e] - split_dot(
+                        (ph[left], pl_[left]), (ph[right], pl_[right]), NT
+                    )
                 for act in between.get(at, ()):
                     act()
 
@@ -121,33 +128,37 @@
     return min(blocks, per_owner)
 
 
-def solve_sides(l_ref, w_ref, br_ref, bc_ref, xh, xl, lh, ll):
-    n = l_ref.shape[0]
-    blocks = br_ref.shape[0] // BLOCK
-    few = 2
-    tile = few * BLOCK
-    sides = (br_ref, bc_ref)
+def invert_pairs(l_ref, w_ref, lh, ll, wh, wl):
+    pair = 2 * BLOCK
     lh[...], ll[...] = parts(l_ref[...])
-    pair = 2 * BLOCK
-    for k in range(n // pair):
+    for k in range(l_ref.shape[0] // pair):
         low, high = k * pair, k * pair + pair
         wa, wb = w_ref[2 * k], w_ref[2 * k + 1]
         across = l_ref[low + BLOCK : high, low : low + BLOCK]
-        wk = parts(square(wa, -full_dot(wb, full_dot(across, wa, NN), NN), wb))
-
-        def solve(i, carry, low=low, high=high, wk=wk):
-            o = pl.multiple_of(i * tile, tile)
-            for side, b in enumerate(sides):
-                rest = b[pl.ds(o, tile), low:high]
-                at = pl.ds(side * blocks + i * few, few)
-                if low:
-                    left = tuple(x[at, :, :low].reshape(tile, low) for x in (xh, xl))
-                    rest = rest - split_dot(left, (lh[low:high, :low], ll[low:high, :low]), NT)
-                x = split_dot(parts(rest), wk, NT)
-                for ref, value in zip((xh, xl), parts(x)):
-                    ref[at, :, low:high] = value.reshape(few, BLOCK, pair)
-                if side == 0:
-                    br_ref[pl.ds(o, tile), low:high] = x
+        wh[k], wl[k] = parts(square(wa, -full_dot(wb, full_dot(across, wa, NN), NN), wb))
+
+
+def solve_rows(b_ref, xh, xl, lh, ll, wh, wl, keep):
+    n = lh.shape[0]
+    blocks = xh.shape[0]
+    grain = b_ref.shape[1]
+    few = next(f for f in (2, 3, 1) if blocks % f == 0)
+    tile, pair = few * BLOCK, 2 * BLOCK
+    for k in range(n // pair):
+        low, high = k * pair, k * pair + pair
+
+        def solve(i, carry, k=k, low=low, high=high):
+            at = pl.ds(i * few, few)
+            from_at = pl.ds(i * (tile // grain), tile // grain)
+            rest = b_ref[from_at, :, low:high].reshape(tile, pair)
+            if low:
+                left = tuple(x[at, :, :low].reshape(tile, low) for x in (xh, xl))
+                rest = rest - split_dot(left, (lh[low:high, :low], ll[low:high, :low]), NT)
+            x = split_dot(parts(rest), (wh[k], wl[k]), NT)
+            for ref, value in zip((xh, xl), parts(x)):
+                ref[at, :, low:high] = value.reshape(few, BLOCK, pair)
+            if keep:
+                b_ref[from_at, :, low:high] = x.reshape(tile // grain, grain, pair)
             return carry
 
         lax.fori_loop(0, blocks // few, solve, 0)
@@ -156,27 +167,35 @@
 def front_kernel(
     rows, columns, owners, sure, quarter, map_ref, d_ref, x_ref, t_ref,
     factor_ref, panel_ref, piece_ref, need_ref,
-    a, w, br, bc, xh, xl, lh, ll, t, stage, x_send, x_recv,
+    a, w, br, side, xh, xl, yh, yl, lh, ll, wh, wl, t, stage, x_send, x_recv,
     local, line_send, line_recv, far_send, far_recv, near_send, near_recv,
     b_send, b_recv, c_send, c_recv,
 ):
     child = lax.axis_index("wide")
     row, column = lax.axis_index("grow"), lax.axis_index("gcol")
-    q = br.shape[0]
+    q = br.shape[0] * br.shape[1]
     blocks = q // BLOCK
+    grain = br.shape[1]
+    bc = side.at[pl.ds(0, q // grain)]
+    half = a.shape[1] // 2
     per_owner = quarter // owners
     far_row = lax.rem(row + rows // 2, rows)
     near_row = row + 1 - 2 * lax.rem(row, 2)
     right, left = {"gcol": column + 1}, {"gcol": column - 1}
     far, near = {"grow": far_row}, {"grow": near_row}
-    share, part = d_ref.shape[0], x_ref.shape[0]
+    share, part = d_ref.shape[0], x_ref.shape[0] * x_ref.shape[1]
     has_left, has_right = column > 0, column < columns - 1
 
     def band(r, c):
         return a.at[pl.ds(pl.multiple_of((r * columns + c) * share, share), share)]
 
+    def cross(r, c):
+        side_of = pl.multiple_of((r // (rows // 2)) * half, half)
+        rows_of = pl.ds(pl.multiple_of((r * columns + c) * share, share), share)
+        return a.at[rows_of, pl.ds(side_of, half)]
+
     def piece(ref, c):
-        return ref.at[pl.ds(pl.multiple_of(c * part, part), part)]
+        return ref.at[pl.ds(c * (part // grain), part // grain)]
 
     def remote(ref, send, recv, to):
         return pltpu.make_async_remote_copy(
@@ -227,7 +246,7 @@
             pl.when(there)(functools.partial(act, c))
 
     def spread(c):
-        remote(band(row, c), far_send.at[c], far_recv.at[c], far).start()
+        remote(cross(row, c), far_send.at[c], far_recv.at[c], far).start()
         remote(band(row, c), near_send.at[0, c], near_recv.at[0, c], near).start()
 
     pass_on(band(row, column), line_send, line_recv, column)
@@ -239,8 +258,8 @@
         spread(c)
 
     def crossed(c):
-        remote(band(far_row, c), far_send.at[c], far_recv.at[c], far).wait_recv()
-        remote(band(far_row, c), near_send.at[1, c], near_recv.at[1, c], near).start()
+        remote(cross(far_row, c), far_send.at[c], far_recv.at[c], far).wait_recv()
+        remote(cross(far_row, c), near_send.at[1, c], near_recv.at[1, c], near).start()
 
     at_distance(1, arrived)
     crossed(column)
@@ -252,11 +271,11 @@
     near_far_row = lax.rem(near_row + rows // 2, rows)
     for c in range(columns):
         remote(band(near_row, c), near_send.at[0, c], near_recv.at[0, c], near).wait_recv()
-        remote(band(near_far_row, c), near_send.at[1, c], near_recv.at[1, c], near).wait_recv()
+        remote(cross(near_far_row, c), near_send.at[1, c], near_recv.at[1, c], near).wait_recv()
     for c in range(columns):
-        remote(band(row, c), far_send.at[c], far_recv.at[c], far).wait_send()
+        remote(cross(row, c), far_send.at[c], far_recv.at[c], far).wait_send()
         remote(band(row, c), near_send.at[0, c], near_recv.at[0, c], near).wait_send()
-        remote(band(far_row, c), near_send.at[1, c], near_recv.at[1, c], near).wait_send()
+        remote(cross(far_row, c), near_send.at[1, c], near_recv.at[1, c], near).wait_send()
         passed(band(row, c), line_send, line_recv, c)
 
     root = row == column
@@ -285,14 +304,27 @@
             remote(piece(bc, c), c_send.at[1, c], c_recv.at[c], near).start()
 
     give(column)
+
+    @pl.when(row < rows // 2)
+    def _():
+        for i in range(0, half, BLOCK):
+            for j in range(0, half, BLOCK):
+                a[half + i : half + i + BLOCK, j : j + BLOCK] = (
+                    a[j : j + BLOCK, half + i : half + i + BLOCK].T
+                )
+
     between = {}
     between[1] = [functools.partial(at_distance, 1, take)]
     between[2] = [functools.partial(forward, column)]
-    between[3] = [functools.partial(at_distance, 2, take)]
-    between[4] = [functools.partial(at_distance, 1, forward)]
-    between[5] = [functools.partial(at_distance, d, take) for d in range(3, columns)]
-    between[6] = [functools.partial(at_distance, d, forward) for d in range(2, columns)]
+    between[4] = [functools.partial(at_distance, 2, take)]
+    between[5] = [functools.partial(at_distance, 1, forward)]
     factor_in_place(a, w, between)
+    for d in range(3, columns):
+        at_distance(d, take)
+    for d in range(2, columns):
+        at_distance(d, forward)
+    factor_ref[...] = a[pl.ds(pl.multiple_of((row * columns + column) * share, share), share), :]
+    invert_pairs(a, w, lh, ll, wh, wl)
     for c in range(columns):
 
         @pl.when(from_near)
@@ -314,9 +346,6 @@
     def _():
         bc[...] = br[...]
 
-
-    factor_ref[...] = a[pl.ds(pl.multiple_of((row * columns + column) * share, share), share), :]
-    solve_sides(a, w, br, bc, xh, xl, lh, ll)
     own_t.wait()
 
     def owner(g, r, b):
@@ -340,20 +369,40 @@
         )
 
     slots = [(d, i) for d in range(1, owners) for i in range(sure)]
-    columns_side = tuple(x[blocks:].reshape(q, x.shape[2]) for x in (xh, xl))
+    picked = [pick(lax.rem(child + d, owners), i) for d, i in slots]
+    each = BLOCK // grain
+    ahead = xh.shape[0] > blocks
+    for s, block in enumerate(picked if ahead else ()):
+        for h in range(each):
+            side[q // grain + s * each + h] = br[block * each + h]
+    if not ahead:
+        solve_rows(br, yh, yl, lh, ll, wh, wl, True)
+    solve_rows(side, xh, xl, lh, ll, wh, wl, False)
+    columns_side = tuple(x[:blocks].reshape(q, x.shape[2]) for x in (xh, xl))
     for first in range(0, len(slots), 2):
-        group = slots[first : first + 2]
-        at = [pick(lax.rem(child + d, owners), i) for d, i in group]
-        sides = tuple(jnp.concatenate([x[p] for p in at], axis=0) for x in (xh, xl))
+        last = min(first + 2, len(slots))
+        count = last - first
+        if ahead:
+            sides = tuple(
+                x[blocks + first : blocks + last].reshape(count * BLOCK, x.shape[2])
+                for x in (xh, xl)
+            )
+        else:
+            sides = tuple(
+                jnp.concatenate([y[block] for block in picked[first:last]], axis=0)
+                for y in (yh, yl)
+            )
         product = split_dot(sides, columns_side, NT)
-        for n, (p, (d, _)) in enumerate(zip(at, group)):
-            stage[first + n] = t[p] - product[n * BLOCK : n * BLOCK + BLOCK, :]
-            give_away(first + n, d).start()
-    panel_ref[...] = br[pl.ds(pl.multiple_of(column * part, part), part), :]
+        for n in range(count):
+            stage[first + n] = t[picked[first + n]] - product[n * BLOCK : n * BLOCK + BLOCK, :]
+            give_away(first + n, slots[first + n][0]).start()
+    if ahead:
+        solve_rows(br, yh, yl, lh, ll, wh, wl, True)
+    panel_ref[...] = br[pl.ds(column * (part // grain), part // grain)].reshape(part, a.shape[1])
     step = 3 if blocks % 3 == 0 else 1
     for first in range(0, blocks, step):
         low, high = first * BLOCK, (first + step) * BLOCK
-        rows_side = tuple(x[first : first + step].reshape(high - low, x.shape[2]) for x in (xh, xl))
+        rows_side = tuple(x[first : first + step].reshape(high - low, x.shape[2]) for x in (yh, yl))
         product = split_dot(rows_side, columns_side, NT)
         for b in range(first, first + step):
             o = b * BLOCK
@@ -378,6 +427,8 @@
     blocks = q // BLOCK
     dma = pltpu.SemaphoreType.DMA
     away = (owners - 1) * sure
+    grain = math.gcd(part, BLOCK)
+    ahead = away if away < blocks else 0
     return pl.pallas_call(
         functools.partial(front_kernel, rows, columns, owners, sure, quarter),
         name="front",
@@ -392,12 +443,16 @@
         scratch_shapes=[
             pltpu.VMEM((n, n), F32),
             pltpu.VMEM((n // BLOCK, BLOCK, BLOCK), F32),
-            pltpu.VMEM((q, n), F32),
-            pltpu.VMEM((q, n), F32),
-            pltpu.VMEM((2 * blocks, BLOCK, n), BF16),
-            pltpu.VMEM((2 * blocks, BLOCK, n), BF16),
+            pltpu.VMEM((q // grain, grain, n), F32),
+            pltpu.VMEM(((q + ahead * BLOCK) // grain, grain, n), F32),
+            pltpu.VMEM((blocks + ahead, BLOCK, n), BF16),
+            pltpu.VMEM((blocks + ahead, BLOCK, n), BF16),
+            pltpu.VMEM((blocks, BLOCK, n), BF16),
+            pltpu.VMEM((blocks, BLOCK, n), BF16),
             pltpu.VMEM((n, n), BF16),
             pltpu.VMEM((n, n), BF16),
+            pltpu.VMEM((n // (2 * BLOCK), 2 * BLOCK, 2 * BLOCK), BF16),
+            pltpu.VMEM((n // (2 * BLOCK), 2 * BLOCK, 2 * BLOCK), BF16),
             pltpu.VMEM((blocks, BLOCK, q), F32),
             pltpu.VMEM((away, BLOCK, q), F32),
             dma((away,)), dma((away,)),
@@ -408,7 +463,9 @@
         compiler_params=pltpu.CompilerParams(
             vmem_limit_bytes=56 << 20, collective_id=0, has_side_effects=True
         ),
-    )(row_map, diag, lower, trailing.reshape(blocks, BLOCK, q))
+    )(
+        row_map, diag, lower.reshape(part // grain, grain, n), trailing.reshape(blocks, BLOCK, q)
+    )
 
 
 def rest_kernel(owners, sure, more, quarter, map_ref, piece_ref, out_ref, stage, send, recv):
@@ -456,12 +513,12 @@
         out_specs=VMEM,
         scratch_shapes=[pltpu.VMEM(shape, F32), dma((away,)), dma((away,))],
         compiler_params=pltpu.CompilerParams(
-            vmem_limit_bytes=12 << 20, collective_id=1, has_side_effects=True
+            vmem_limit_bytes=12 << 20, collective_id=more, has_side_effects=True
         ),
     )(row_map, pieces)
 
 
-def add_kernel(owners, sure, map_ref, parent_ref, *refs):
+def add_kernel(owners, sure, more, map_ref, parent_ref, *refs):
     pieces, out_ref = refs[:-1], refs[-1]
     p = pl.program_id(0)
     per_owner = pl.num_programs(0)
@@ -489,8 +546,6 @@
                 at = pl.ds(pl.multiple_of(to * BLOCK, BLOCK), BLOCK)
                 out_ref[0, :, at] += ref[index, :, b * BLOCK : b * BLOCK + BLOCK]
 
-        more = most_slots(blocks, per_owner) - sure
-
         @pl.when((block >= 0) & ((g == child) | (slot < sure)))
         def _():
             put(pieces[0], jnp.where(g == child, block, blocks + away * sure + slot))
@@ -506,11 +561,11 @@
     lax.fori_loop(0, owners, add, 0)
 
 
-def add_call(row_map, parent, pieces, owners, sure):
+def add_call(row_map, parent, pieces, owners, sure, more):
     _, rows, width = parent.shape
     block = pl.BlockSpec((1, BLOCK, width), lambda p: (0, p, 0))
     return pl.pallas_call(
-        functools.partial(add_kernel, owners, sure),
+        functools.partial(add_kernel, owners, sure, more),
         name="extend_add",
         out_shape=jax.ShapeDtypeStruct(parent.shape, F32),
         grid=(rows // BLOCK,),
@@ -531,14 +586,15 @@
         row_map, diag_block[0], lower_block[0], trailing_block[0], rows, columns, owners, sure, quarter,
     )
 
-    def few():
-        return add_call(row_map, parent_front, (pieces,), owners, sure)
-
-    def many():
-        rest = rest_call(row_map, pieces, owners, sure, most - sure, quarter)
-        return add_call(row_map, parent_front, (pieces, rest), owners, sure)
-
-    parent = lax.cond(need[0] > sure, many, few) if most > sure else few()
+    def finish(more):
+        def run():
+            extra = (rest_call(row_map, pieces, owners, sure, more, quarter),) if more else ()
+            return add_call(row_map, parent_front, (pieces,) + extra, owners, sure, more)
+
+        return run
+
+    branches = [finish(more) for more in range(most - sure + 1)]
+    parent = lax.switch(jnp.clip(need[0] - sure, 0, most - sure), branches)
     return (factor[None], panel[None], parent)
 
 

time: 163 us -> 153 us (0.939)
  Pallas kernels: 160 us -> 150 us
    pallas_call x1, Pallas kernels: 150 us -> 140 us  [front_call(): pl.pallas_call(functools.partial(front_kernel, rows, columns, owners, sur...]
where the time goes in v2:
time: 153 us
  Pallas kernels  150 us (98%)
  local copies, waits for them, and re-layouts  1.59 us (1%)
    pallas_call x1, Pallas kernels, front_call(): pl.pallas_call(functools.partial(front_kernel, rows, columns, owners, sur...  140 us
    pallas_call x1, Pallas kernels, add_call(): pl.pallas_call(functools.partial(add_kernel, owners, sure, more), name='e...  9.89 us

profile of v2, /device:TPU:4, one launch (start us, length us, event | category | flops | bytes accessed | tf_op | source)
XLA Modules:
  0.0 153.1 jit_solution(11616498529028227265)
XLA Ops:
  0.6 140.3 %front.1 = (f32[64,1024]{1,0:T(8,128)}, f32[192,1024]{1,0:T(8,128)}, f32[10,128,768]{2,1,0:T(8,128)S(1)}, s32[1]{0:T(128)}) custom-call(s32[2,24]{1,0:T(2,128)} %map_ref.1, f32[64,1024]{1,0:T(8,128)} %bitcast.9, f32[3,64,1024]{2,1,0:T(8,128)} %bitcast.8, f32[6,128,768]{2,1,0:T(8,128)} %bitcast.6), custom_call_target="tpu_custom_call" | custom-call | tf_op jit(solution)/shard_map/front/pallas_call | solution.py:432
  141.6 0.0 copy-start.1
  141.6 0.0 copy-start
  141.6 9.9 %conditional.1 = (f32[1,1024,2048]{2,1,0:T(8,128)}) conditional(s32[]{:T(128)} %bitcast.5, (s32[2,24]{1,0:T(2,128)}, f32[1,1024,2048]{2,1,0:T(8,128)}, f32[10,128,768]{2,1,0:T(8,128)S(1)}) %tuple.17, (s32[2,24]{1,0:T(2,128)}, f32[10,128,768]{2,1,0:T(8,128)S(1)}, f32[1,1024,2048]{2,1,0:T(8,128)}) %tuple.18, (s32[2,24]{1,0:T(2,128)}, ...), branch_computations={%region_0.1_spmd, %region_1.2_spmd, %region_2.3_spmd} | conditional | bytes 8 | solution.py:597
  141.6 9.9 %extend_add.3 = f32[1,1024,2048]{2,1,0:T(8,128)} custom-call(s32[2,24]{1,0:T(2,128)} %get-tuple-element.18.map_ref, f32[1,1024,2048]{2,1,0:T(8,128)} %get-tuple-element.19.parent_ref, f32[10,128,768]{2,1,0:T(8,128)S(1)} %get-tuple-element.24.refs_0_), custom_call_target="tpu_custom_call" | custom-call | tf_op jit(solution)/shard_map/cond/branch_0_fun/extend_add/pallas_call | solution.py:567
  151.5 0.0 copy-done.1
  151.5 0.7 copy.13
  152.2 0.0 copy-done
  152.2 0.9 copy.14
Async XLA Ops:
  141.6 9.9 %copy-start.1 = (f32[64,1024]{1,0:T(8,128)S(1)}, f32[64,1024]{1,0:T(8,128)}, u32[]{:S(2)}) copy-start(f32[64,1024]{1,0:T(8,128)} %get-tuple-element.38) | copy-start | bytes 786436
  141.6 10.6 %copy-start = (f32[192,1024]{1,0:T(8,128)S(1)}, f32[192,1024]{1,0:T(8,128)}, u32[]{:S(2)}) copy-start(f32[192,1024]{1,0:T(8,128)} %get-tuple-element.39) | copy-start | bytes 2359300
